TPU v7x, 256 devices: a whole 4x4x8 slice. The times are simulated.
256 devices in a mesh: dp: 2 (over core), tm: 32 (over z, y), space: 4 (over x).
Axes of the slice: x: 4, y: 4, z: 8, core: 2. Of those that a mesh axis runs over, the one named last changes fastest.
Arguments:
- latents: bfloat16 [2, 64, 8, 80, 512], P('dp', 'tm', 'space'), may hold values from -6 to 6
- norm_gain: float32 [512], replicated, may hold values from 0.25 to 1.75
- kernel: bfloat16 [13824, 512], P(None, 'dp'), may hold values from -0.0546875 to 0.0546875
- conv_bias: float32 [512], replicated, may hold values from -3 to 3
- out_grad: bfloat16 [2, 64, 8, 80, 512], P('dp', 'tm', 'space'), may hold values from -6 to 6
Outputs:
- block_out: bfloat16 [2, 64, 8, 80, 512], P('dp', 'tm', 'space')
- latent_grad: bfloat16 [2, 64, 8, 80, 512], P('dp', 'tm', 'space')
- kernel_grad: float32 [13824, 512], P('tm', 'dp')
- gain_grad: float32 [512], replicated
- bias_grad: float32 [512], replicated
All inputs are finite; a program needn't handle non-finite values.
Results may differ from a plain program's by a relative error of at most 0.0029.
Values may be sent and summed in bfloat16 or wider, within the bound.
No kernel may reach another device: no remote copies, remote signals or barrier semaphores. Data moves between devices by JAX's collectives and lax.ppermute only.
A program may use at most 128 MiB of HBM per device.

v0:
```python
import jax
import jax.numpy as jnp
from jax import lax
from jax.sharding import PartitionSpec as P


def shifted(block, axis, distance):
    devices = range(lax.axis_size(axis))
    route = [(i - distance, i) for i in devices if i - distance in devices]
    return lax.ppermute(block, axis, route)


def padded(block, sides, width):
    for axis, dim in sides:
        count = lax.axis_size(axis)
        forward = [(i, i + 1) for i in range(count - 1)]
        backward = [(target, source) for source, target in forward]
        low = lax.ppermute(
            lax.slice_in_dim(block, block.shape[dim] - width, None, axis=dim), axis, forward
        )
        high = lax.ppermute(lax.slice_in_dim(block, 0, width, axis=dim), axis, backward)
        block = jnp.concatenate([low, block, high], axis=dim)
    return block


def tap_columns(extended, frame_count, row_count, col_count, flipped):
    pieces = []
    for tap_t in range(3):
        for tap_h in range(3):
            for tap_w in range(3):
                if flipped:
                    start_t, start_h, start_w = (2 - tap_t, 2 - tap_h, 2 - tap_w)
                else:
                    start_t, start_h, start_w = (tap_t, tap_h, tap_w)
                pieces.append(
                    extended[
                        :,
                        start_t : start_t + frame_count,
                        start_h : start_h + row_count,
                        start_w : start_w + col_count,
                        :,
                    ]
                )
    stacked = jnp.concatenate(pieces, axis=-1)
    return stacked.reshape(-1, stacked.shape[-1])


def pad_columns(extended):
    return jnp.pad(extended, ((0, 0), (0, 0), (0, 0), (1, 1), (0, 0)))


def on_device(latents, norm_gain, kernel, conv_bias, out_grad):
    chans = latents.shape[-1]
    half_cols = kernel.shape[1]
    clip_local, frame_count, row_count, col_count = (
        latents.shape[0],
        latents.shape[1],
        latents.shape[2],
        latents.shape[3],
    )
    cell_total = (
        clip_local
        * frame_count
        * row_count
        * col_count
        * lax.axis_size("dp")
        * lax.axis_size("tm")
        * lax.axis_size("space")
    )
    grad_scale = 1.0 / jnp.sqrt(jnp.float32(cell_total))
    floats = latents.astype(jnp.float32)
    scale = lax.rsqrt(jnp.mean(floats * floats, axis=-1, keepdims=True) + 1e-06)
    normed = floats * scale
    pre_act = normed * norm_gain
    act = jax.nn.silu(pre_act).astype(jnp.bfloat16)
    grad_pair = lax.all_to_all(out_grad, "dp", split_axis=4, concat_axis=0, tiled=True)
    earlier = shifted(act, "tm", 1)
    joined = jnp.concatenate([earlier, act], axis=1)
    act_ext = padded(joined, (("space", 2),), 1)
    later = shifted(grad_pair, "tm", -1)
    joined_grad = jnp.concatenate([grad_pair, later], axis=1)
    grad_ext = padded(joined_grad, (("space", 2),), 1)
    act_pair = lax.all_gather(act_ext, "dp", axis=0, tiled=True)
    pair_clips = act_pair.shape[0]
    act_taps = tap_columns(pad_columns(act_pair), frame_count, row_count, col_count, False)
    conv_part = jnp.dot(act_taps, kernel, preferred_element_type=jnp.float32)
    conv_part = conv_part.reshape(pair_clips, frame_count, row_count, col_count, half_cols)
    conv = lax.all_to_all(conv_part, "dp", split_axis=0, concat_axis=4, tiled=True)
    block_out = (floats + conv + conv_bias).astype(jnp.bfloat16)
    kernel_local = (
        lax.dot_general(
            act_taps,
            grad_pair.reshape(-1, half_cols),
            (((0,), (0,)), ((), ())),
            preferred_element_type=jnp.float32,
        )
        * grad_scale
    )
    flipped_kernel = jnp.transpose(kernel.reshape(-1, chans, half_cols), (0, 2, 1)).reshape(
        -1, chans
    )
    grad_taps = tap_columns(pad_columns(grad_ext), frame_count, row_count, col_count, True)
    partial_grad = jnp.dot(grad_taps, flipped_kernel, preferred_element_type=jnp.float32)
    partial_grad = partial_grad.reshape(pair_clips, frame_count, row_count, col_count, chans)
    act_grad = lax.psum_scatter(partial_grad, "dp", scatter_dimension=0, tiled=True)
    grads = out_grad.astype(jnp.float32)
    bias_local = jnp.sum(grads.reshape(-1, chans), axis=0) * grad_scale
    sig = jax.nn.sigmoid(pre_act)
    pre_grad = act_grad * sig * (1.0 + pre_act * (1.0 - sig))
    gain_local = jnp.sum((pre_grad * normed).reshape(-1, chans), axis=0) * grad_scale
    normed_grad = pre_grad * norm_gain
    latent_grad = grads + scale * (
        normed_grad - normed * jnp.mean(normed_grad * normed, axis=-1, keepdims=True)
    )
    gain_grad, bias_grad = lax.psum((gain_local, bias_local), ("dp", "tm", "space"))
    row_part = lax.psum_scatter(kernel_local, "tm", scatter_dimension=0, tiled=True)
    kernel_grad = lax.psum(row_part, "space")
    return (block_out, latent_grad.astype(jnp.bfloat16), kernel_grad, gain_grad, bias_grad)


def solution(mesh):
    in_specs = (
        P("dp", "tm", "space", None, None),
        P(),
        P(None, "dp"),
        P(),
        P("dp", "tm", "space", None, None),
    )
    out_specs = (
        P("dp", "tm", "space", None, None),
        P("dp", "tm", "space", None, None),
        P("tm", "dp"),
        P(),
        P(),
    )
    return jax.shard_map(
        on_device, mesh=mesh, in_specs=in_specs, out_specs=out_specs, check_vma=False
    )
```

profile of v0, /device:TPU:8, one launch (start us, length us, event | category | flops | bytes accessed | tf_op | source)
XLA Modules:
  0.0 441.9 jit_solution(11372110334327910266)
XLA Ops:
  7.2 1.3 copy.20
  8.5 4.2 all_to_all.36
  12.6 0.4 copy.22
  13.0 4.1 collective-permute-start.3
  17.1 7.6 %collective-permute-done.3 = bf16[2,2,2,80,256]{4,3,2,1,0:T(8,128)(2,1)S(1)} collective-permute-done((bf16[2,2,2,80,256]{4,3,2,1,0:T(8,128)(2,1)S(1)}, bf16[2,2,2,80,256]{4,3,2,1,0:T(8,128)(2,1)S(1)}, u32[]{:S(2)}, u32[]{:S(2)}) %collective-permute-start.3) | collective-permute-done | bytes 327712 | tf_op jit(solution)/shard_map/ppermute | solution.py:10
  24.7 3.4 collective-permute-start.4
  28.2 1.3 collective-permute-start.5
  29.5 10.3 %copy.23 = bf16[27,256,512]{2,1,0:T(8,128)(2,1)} copy(bf16[27,256,512]{1,2,0:T(8,128)(2,1)} %bitcast.37) | data formatting | bytes 14155776 | tf_op jit(solution)/shard_map/transpose | solution.py:99
  39.8 0.7 select_maximum_fusion
  42.0 0.9 slice-done
  42.9 1.1 slice-done.1
  44.0 5.8 %fusion.31 = f32[2,2,2,80,512]{4,3,2,1,0:T(8,128)} fusion(bf16[2,2,2,80,6912]{4,3,2,1,0:T(8,128)(2,1)S(1)} %slice_dynamic-update-slice_fusion.27, bf16[6912,512,1,1,1]{1,0,4,3,2:T(8,128)(2,1)S(1)} %bitcast.40), kind=kOutput, calls=%fused_computation.109 | convolution fusion | flops 4529848320 | bytes 17235968 | tf_op jit(solution)/shard_map/dot_general | solution.py:103
  49.9 0.2 fusion.24
  50.1 20.0 %reduce-scatter.3.cloned.1.call-done = f32[1,2,2,80,512]{4,3,2,1,0:T(8,128)} async-done(((f32[2,2,2,80,512]{4,3,2,1,0:T(8,128)}), f32[1,2,2,80,512]{4,3,2,1,0:T(8,128)}) %reduce-scatter.3.cloned.1.call-update) | async-done | bytes 655376 | tf_op jit(solution)/shard_map/reduce_scatter | solution.py:105
  70.1 1.6 fusion.23
  71.7 2.4 fusion.13
  74.1 3.4 collective-permute-start
  77.5 8.2 %collective-permute-done = bf16[1,2,2,80,512]{4,3,2,1,0:T(8,128)(2,1)S(1)} collective-permute-done((bf16[1,2,2,80,512]{4,3,2,1,0:T(8,128)(2,1)S(1)}, bf16[1,2,2,80,512]{4,3,2,1,0:T(8,128)(2,1)S(1)}, u32[]{:S(2)}, u32[]{:S(2)}) %collective-permute-start) | collective-permute-done | bytes 327712 | tf_op jit(solution)/shard_map/ppermute | solution.py:10
  85.8 3.4 collective-permute-start.1
  89.2 1.3 collective-permute-start.2
  90.5 5.1 %collective-permute-done.1 = bf16[1,4,1,80,512]{4,3,2,1,0:T(8,128)(2,1)S(1)} collective-permute-done((bf16[1,4,1,80,512]{4,3,2,1,0:T(8,128)(2,1)S(1)}, bf16[1,4,1,80,512]{4,3,2,1,0:T(8,128)(2,1)S(1)}, u32[]{:S(2)}, u32[]{:S(2)}) %collective-permute-start.1) | collective-permute-done | bytes 327712 | tf_op jit(solution)/shard_map/ppermute | solution.py:18
  95.6 4.1 collective-permute-done.2
  99.7 1.2 pad_maximum_fusion
  101.0 0.2 reduce-scatter.5.cloned.1.call-start
  101.2 18.5 %all-gather.2.cloned.1.call-done = bf16[2,4,4,80,512]{4,3,2,1,0:T(8,128)(2,1)} async-done(((bf16[1,4,4,80,512]{4,3,2,1,0:T(8,128)(2,1)}), bf16[2,4,4,80,512]{4,3,2,1,0:T(8,128)(2,1)}) %all-gather.2.cloned.1.call-update) | async-done | bytes 2621456 | tf_op jit(solution)/shard_map/all_gather | solution.py:83
  119.7 1.4 slice_dynamic-update-slice_fusion.26
  121.0 1.1 slice_dynamic-update-slice_fusion.8
  122.2 1.2 slice_dynamic-update-slice_fusion.25
  123.4 0.2 slice_dynamic-update-slice_fusion.24
  123.6 0.2 slice_dynamic-update-slice_fusion.23
  123.8 0.2 slice_dynamic-update-slice_fusion.22
  124.0 0.2 slice_dynamic-update-slice_fusion.21
  124.4 0.2 slice_dynamic-update-slice_fusion.19
  124.5 0.2 slice_dynamic-update-slice_fusion.18
  124.8 0.2 slice_dynamic-update-slice_fusion.17
  125.1 0.2 slice_dynamic-update-slice_fusion.15
  125.5 0.2 slice_dynamic-update-slice_fusion.13
  125.9 0.2 slice_dynamic-update-slice_fusion.11
  126.3 0.2 slice_dynamic-update-slice_fusion.9
  126.4 6.1 %copy-done.3 = bf16[2,2,2,80,13824]{4,3,2,1,0:T(8,128)(2,1)} copy-done((bf16[2,2,2,80,13824]{4,3,2,1,0:T(8,128)(2,1)}, bf16[2,2,2,80,13824]{4,3,2,1,0:T(8,128)(2,1)S(1)}, u32[]{:S(2)}) %copy-start.3) | copy-done | bytes 17694744
  132.5 9.0 %convolution_multiply_fusion = f32[13824,256]{1,0:T(8,128)} fusion(bf16[640,13824]{1,0:T(8,128)(2,1)S(1)} %bitcast.44, bf16[640,256]{1,0:T(8,128)(2,1)S(1)} %bitcast.36), kind=kOutput, calls=%fused_computation | convolution fusion | flops 4533387264 | bytes 32178176 | tf_op jit(solution)/shard_map/dot_general | solution.py:91
  141.6 77.4 %all-reduce.2 = (f32[512]{0:T(512)}, f32[512]{0:T(512)}) all-reduce(f32[512]{0:T(512)S(1)} %broadcast_multiply_fusion.1, f32[512]{0:T(512)S(1)} %broadcast_multiply_fusion), channel_id=1, replica_groups=mesh['dp'=2,'tm'=32,'space'=4] {'dp','tm','space'}, use_global_device_ids=true, to_apply=%region_6.7 | all-reduce | flops 1024 | bytes 8192 | tf_op jit(solution)/shard_map/psum | solution.py:115
  219.0 165.6 %reduce-scatter.5.cloned.1.call-done = f32[432,256]{1,0:T(8,128)} async-done(((f32[13824,256]{1,0:T(8,128)}), f32[432,256]{1,0:T(8,128)}) %reduce-scatter.5.cloned.1.call-update) | async-done | bytes 442384 | tf_op jit(solution)/shard_map/reduce_scatter | solution.py:116
  384.6 10.5 %fusion = f32[2,2,2,80,256]{4,3,2,1,0:T(8,128)S(1)} fusion(bf16[2,2,2,80,13824]{4,3,2,1,0:T(8,128)(2,1)} %copy-done.3, bf16[13824,256]{1,0:T(8,128)(2,1)} %param.7), kind=kOutput, calls=%fused_computation.1 | convolution fusion | flops 4529848320 | bytes 25427968 | tf_op jit(solution)/shard_map/dot_general | solution.py:86
  395.2 4.3 all_to_all.37
  399.5 0.8 fusion.26
  400.3 33.2 %all-reduce.5.cloned.1.call-done = f32[432,256]{1,0:T(8,128)} async-done(((f32[432,256]{1,0:T(8,128)}), f32[432,256]{1,0:T(8,128)}) %all-reduce.5.cloned.1.call-update) | async-done | bytes 442384 | tf_op jit(solution)/shard_map/psum | solution.py:117
  433.5 1.8 copy.82
  (71 shorter events, 2.9 us)
Async XLA Ops:
  7.2 62.9 %reduce-scatter.3.cloned.1.call-start = ((), (), s32[]{:S(2)}) async-start(), calls=%async_computation.5 | async-start | bytes 1966080 | tf_op jit(solution)/shard_map/reduce_scatter | solution.py:105
  13.0 11.6 %collective-permute-start.3 = (bf16[2,2,2,80,256]{4,3,2,1,0:T(8,128)(2,1)S(1)}, bf16[2,2,2,80,256]{4,3,2,1,0:T(8,128)(2,1)S(1)}, u32[]{:S(2)}, u32[]{:S(2)}) collective-permute-start(bf16[2,2,2,80,256]{4,3,2,1,0:T(8,128)(2,1)S(1)} %bitcast.31), channel_id=1, source_target_pairs={{4,0},{8,4},{12,8},{16,12},{20,16},{24,20},{28,24},{32,28},{36,32}... | collective-permute-start | bytes 983048 | tf_op jit(solution)/shard_map/ppermute | solution.py:10
  24.7 15.0 %collective-permute-start.4 = (bf16[2,4,1,80,256]{4,3,2,1,0:T(8,128)(2,1)S(1)}, bf16[2,4,1,80,256]{4,3,2,1,0:T(8,128)(2,1)S(1)}, u32[]{:S(2)}, u32[]{:S(2)}) collective-permute-start(bf16[2,4,1,80,256]{4,3,2,1,0:T(8,128)(2,1)S(1)} %get-tuple-element.11), channel_id=1, source_target_pairs={{0,1},{1,2},{2,3},{4,5},{5,6},{6,7},{8,9},{9,10},{10,11},{12,13},{... | collective-permute-start | bytes 983048 | tf_op jit(solution)/shard_map/ppermute | solution.py:18
  28.2 11.6 %collective-permute-start.5 = (bf16[2,4,1,80,256]{4,3,2,1,0:T(8,128)(2,1)S(1)}, bf16[2,4,1,80,256]{4,3,2,1,0:T(8,128)(2,1)S(1)}, u32[]{:S(2)}, u32[]{:S(2)}) collective-permute-start(bf16[2,4,1,80,256]{4,3,2,1,0:T(8,128)(2,1)S(1)} %get-tuple-element.12), channel_id=1, source_target_pairs={{1,0},{2,1},{3,2},{5,4},{6,5},{7,6},{9,8},{10,9},{11,10},{13,12},{... | collective-permute-start | bytes 983048 | tf_op jit(solution)/shard_map/ppermute | solution.py:21
  40.7 2.2 slice-start
  41.4 2.6 slice-start.1
  44.0 5.9 %copy-start.1 = (bf16[1,2,2,80,512]{4,3,2,1,0:T(8,128)(2,1)S(1)}, bf16[1,2,2,80,512]{4,3,2,1,0:T(8,128)(2,1)}, u32[]{:S(2)}) copy-start(bf16[1,2,2,80,512]{4,3,2,1,0:T(8,128)(2,1)} %param.5) | copy-start | bytes 983044
  44.0 26.1 %copy-start.4 = (f32[512]{0:T(512)S(1)}, f32[512]{0:T(512)}, u32[]{:S(2)}) copy-start(f32[512]{0:T(512)} %param.6) | copy-start | bytes 6148
  44.0 27.7 %copy-start.2 = (bf16[1,2,2,80,512]{4,3,2,1,0:T(8,128)(2,1)S(1)}, bf16[1,2,2,80,512]{4,3,2,1,0:T(8,128)(2,1)}, u32[]{:S(2)}) copy-start(bf16[1,2,2,80,512]{4,3,2,1,0:T(8,128)(2,1)} %param.9) | copy-start | bytes 983044
  49.8 69.8 %all-gather.2.cloned.1.call-start = ((), (), s32[]{:S(2)}) async-start(), calls=%async_computation.4 | async-start | bytes 3932160 | tf_op jit(solution)/shard_map/all_gather | solution.py:83
  74.1 11.6 %collective-permute-start = (bf16[1,2,2,80,512]{4,3,2,1,0:T(8,128)(2,1)S(1)}, bf16[1,2,2,80,512]{4,3,2,1,0:T(8,128)(2,1)S(1)}, u32[]{:S(2)}, u32[]{:S(2)}) collective-permute-start(bf16[1,2,2,80,512]{4,3,2,1,0:T(8,128)(2,1)S(1)} %get-tuple-element.16), channel_id=1, source_target_pairs={{0,4},{4,8},{8,12},{12,16},{16,20},{20,24},{24,28},{28,32},{32,36}... | collective-permute-start | bytes 983048 | tf_op jit(solution)/shard_map/ppermute | solution.py:10
  85.8 9.8 %collective-permute-start.1 = (bf16[1,4,1,80,512]{4,3,2,1,0:T(8,128)(2,1)S(1)}, bf16[1,4,1,80,512]{4,3,2,1,0:T(8,128)(2,1)S(1)}, u32[]{:S(2)}, u32[]{:S(2)}) collective-permute-start(bf16[1,4,1,80,512]{4,3,2,1,0:T(8,128)(2,1)S(1)} %get-tuple-element.13), channel_id=1, source_target_pairs={{0,1},{1,2},{2,3},{4,5},{5,6},{6,7},{8,9},{9,10},{10,11},{12,13},{... | collective-permute-start | bytes 983048 | tf_op jit(solution)/shard_map/ppermute | solution.py:18
  89.2 10.5 %collective-permute-start.2 = (bf16[1,4,1,80,512]{4,3,2,1,0:T(8,128)(2,1)S(1)}, bf16[1,4,1,80,512]{4,3,2,1,0:T(8,128)(2,1)S(1)}, u32[]{:S(2)}, u32[]{:S(2)}) collective-permute-start(bf16[1,4,1,80,512]{4,3,2,1,0:T(8,128)(2,1)S(1)} %get-tuple-element.14), channel_id=1, source_target_pairs={{1,0},{2,1},{3,2},{5,4},{6,5},{7,6},{9,8},{10,9},{11,10},{13,12},{... | collective-permute-start | bytes 983048 | tf_op jit(solution)/shard_map/ppermute | solution.py:21
  101.0 283.7 %reduce-scatter.5.cloned.1.call-start = ((), (), s32[]{:S(2)}) async-start(), calls=%async_computation.6 | async-start | bytes 14598144 | tf_op jit(solution)/shard_map/reduce_scatter | solution.py:116
  119.6 3.8 copy-start
  126.4 6.1 %copy-start.3 = (bf16[2,2,2,80,13824]{4,3,2,1,0:T(8,128)(2,1)}, bf16[2,2,2,80,13824]{4,3,2,1,0:T(8,128)(2,1)S(1)}, u32[]{:S(2)}) copy-start(bf16[2,2,2,80,13824]{4,3,2,1,0:T(8,128)(2,1)S(1)} %slice_dynamic-update-slice_fusion.9) | copy-start | bytes 53084164
  141.5 292.0 %all-reduce.5.cloned.1.call-start = ((), (), s32[]{:S(2)}) async-start(), calls=%async_computation.7 | async-start | bytes 884736 | tf_op jit(solution)/shard_map/psum | solution.py:117
  384.6 14.9 %copy-start.5 = (f32[512]{0:T(512)S(1)}, f32[512]{0:T(512)}, u32[]{:S(2)}) copy-start(f32[512]{0:T(512)} %param.8) | copy-start | bytes 6148
Sparse Core Ops, SparseCore 0:
  50.0 20.0 reduce-scatter.2
  101.1 18.5 all-gather.1
  141.6 242.9 reduce-scatter.4
  386.8 46.6 all-reduce.4
where the time goes:
time: 443 us; the launch traced here: 442 us
  waiting for transfers between devices  262 us (59%)
  blocking collectives  85.8 us (19%)
  local copies, waits for them, and re-layouts  29.6 us (7%)
  matrix products  25.3 us (6%)
  starting transfers between devices  17.2 us (4%)
  between operations  14.4 us (3%)
  other arithmetic  7.21 us (2%)
    reduce_scatter x1, waiting for transfers between devices, on_device(): lax.psum_scatter(kernel_local, 'tm', scatter_dimension=0, tiled=True)  166 us
    psum x1, blocking collectives, on_device(): lax.psum((gain_local, bias_local), ('dp', 'tm', 'space'))  77.4 us
    psum x1, waiting for transfers between devices, on_device(): kernel_grad = lax.psum(row_part, 'space')  33.2 us
    reduce_scatter x1, waiting for transfers between devices, on_device(): lax.psum_scatter(partial_grad, 'dp', scatter_dimension=0, tiled=True)  20 us
    unnamed x69, local copies, waits for them, and re-layouts  18.6 us
    all_gather x1, waiting for transfers between devices, on_device(): act_pair = lax.all_gather(act_ext, 'dp', axis=0, tiled=True)  18.5 us
    ppermute x2, waiting for transfers between devices, shifted(): return lax.ppermute(block, axis, route)  15.8 us
    dot_general x1, matrix products, on_device(): conv_part = jnp.dot(act_taps, kernel, preferred_element_type=jnp.float32)  10.5 us
  transfers between devices with their start and end apart: 10, of which 8 were waited for; matrix products, arithmetic and copies ran while one was open for 5% of the time, Pallas kernels for 0%

commit v1 on v0

--- a/solution.py
+++ b/solution.py
@@ -114,7 +114,7 @@
     )
     gain_grad, bias_grad = lax.psum((gain_local, bias_local), ("dp", "tm", "space"))
     row_part = lax.psum_scatter(kernel_local, "tm", scatter_dimension=0, tiled=True)
-    kernel_grad = lax.psum(row_part, "space")
+    kernel_grad = jnp.sum(lax.all_gather(row_part, "space"), axis=0)
     return (block_out, latent_grad.astype(jnp.bfloat16), kernel_grad, gain_grad, bias_grad)
 
 

time: 443 us -> 426 us (0.962)
  waiting for transfers between devices: 262 us -> 245 us
    psum x1 -> x0, waiting for transfers between devices: 33.2 us -> none  [on_device(): kernel_grad = lax.psum(row_part, 'space')]
    all_gather x0 -> x1, waiting for transfers between devices: none -> 15.8 us  [on_device(): kernel_grad = jnp.sum(lax.all_gather(row_part, 'space'), axis=0)]
    unnamed x69 -> x68, local copies, waits for them, and re-layouts: 18.6 us -> 16.8 us
where the time goes in v1:
time: 426 us; the launch traced here: 425 us
  waiting for transfers between devices  245 us (58%)
  blocking collectives  85.7 us (20%)
  local copies, waits for them, and re-layouts  27.8 us (7%)
  matrix products  25.3 us (6%)
  starting transfers between devices  17.2 us (4%)
  between operations  14.4 us (3%)
  other arithmetic  9.61 us (2%)
    reduce_scatter x1, waiting for transfers between devices, on_device(): lax.psum_scatter(kernel_local, 'tm', scatter_dimension=0, tiled=True)  165 us
    psum x1, blocking collectives, on_device(): lax.psum((gain_local, bias_local), ('dp', 'tm', 'space'))  77.3 us
    reduce_scatter x1, waiting for transfers between devices, on_device(): lax.psum_scatter(partial_grad, 'dp', scatter_dimension=0, tiled=True)  20 us
    all_gather x1, waiting for transfers between devices, on_device(): act_pair = lax.all_gather(act_ext, 'dp', axis=0, tiled=True)  18.5 us
    unnamed x68, local copies, waits for them, and re-layouts  16.8 us
    all_gather x1, waiting for transfers between devices, on_device(): kernel_grad = jnp.sum(lax.all_gather(row_part, 'space'), axis=0)  15.8 us
    ppermute x2, waiting for transfers between devices, shifted(): return lax.ppermute(block, axis, route)  15.8 us
    dot_general x1, matrix products, on_device(): conv_part = jnp.dot(act_taps, kernel, preferred_element_type=jnp.float32)  10.5 us
  transfers between devices with their start and end apart: 10, of which 8 were waited for; matrix products, arithmetic and copies ran while one was open for 5% of the time, Pallas kernels for 0%

profile of v1, /device:TPU:8, one launch (start us, length us, event | category | flops | bytes accessed | tf_op | source)
XLA Modules:
  0.0 424.8 jit_solution(3832529822609520405)
XLA Ops:
  7.2 1.3 copy.20
  8.5 4.2 all_to_all.36
  12.6 0.4 copy.22
  13.0 4.1 collective-permute-start.3
  17.1 7.6 %collective-permute-done.3 = bf16[2,2,2,80,256]{4,3,2,1,0:T(8,128)(2,1)S(1)} collective-permute-done((bf16[2,2,2,80,256]{4,3,2,1,0:T(8,128)(2,1)S(1)}, bf16[2,2,2,80,256]{4,3,2,1,0:T(8,128)(2,1)S(1)}, u32[]{:S(2)}, u32[]{:S(2)}) %collective-permute-start.3) | collective-permute-done | bytes 327712 | tf_op jit(solution)/shard_map/ppermute | solution.py:10
  24.7 3.4 collective-permute-start.4
  28.2 1.3 collective-permute-start.5
  29.5 10.3 %copy.23 = bf16[27,256,512]{2,1,0:T(8,128)(2,1)} copy(bf16[27,256,512]{1,2,0:T(8,128)(2,1)} %bitcast.38) | data formatting | bytes 14155776 | tf_op jit(solution)/shard_map/transpose | solution.py:99
  39.8 0.7 select_maximum_fusion
  42.0 0.9 slice-done
  42.9 1.1 slice-done.1
  44.0 5.8 %fusion.31 = f32[2,2,2,80,512]{4,3,2,1,0:T(8,128)} fusion(bf16[2,2,2,80,6912]{4,3,2,1,0:T(8,128)(2,1)S(1)} %slice_dynamic-update-slice_fusion.27, bf16[6912,512,1,1,1]{1,0,4,3,2:T(8,128)(2,1)S(1)} %bitcast.41), kind=kOutput, calls=%fused_computation.109 | convolution fusion | flops 4529848320 | bytes 17235968 | tf_op jit(solution)/shard_map/dot_general | solution.py:103
  49.9 0.2 fusion.24
  50.1 20.0 %reduce-scatter.3.cloned.1.call-done = f32[1,2,2,80,512]{4,3,2,1,0:T(8,128)} async-done(((f32[2,2,2,80,512]{4,3,2,1,0:T(8,128)}), f32[1,2,2,80,512]{4,3,2,1,0:T(8,128)}) %reduce-scatter.3.cloned.1.call-update) | async-done | bytes 655376 | tf_op jit(solution)/shard_map/reduce_scatter | solution.py:105
  70.1 1.6 fusion.23
  71.7 2.4 fusion.13
  74.1 3.4 collective-permute-start
  77.5 8.2 %collective-permute-done = bf16[1,2,2,80,512]{4,3,2,1,0:T(8,128)(2,1)S(1)} collective-permute-done((bf16[1,2,2,80,512]{4,3,2,1,0:T(8,128)(2,1)S(1)}, bf16[1,2,2,80,512]{4,3,2,1,0:T(8,128)(2,1)S(1)}, u32[]{:S(2)}, u32[]{:S(2)}) %collective-permute-start) | collective-permute-done | bytes 327712 | tf_op jit(solution)/shard_map/ppermute | solution.py:10
  85.8 3.4 collective-permute-start.1
  89.2 1.3 collective-permute-start.2
  90.5 5.1 %collective-permute-done.1 = bf16[1,4,1,80,512]{4,3,2,1,0:T(8,128)(2,1)S(1)} collective-permute-done((bf16[1,4,1,80,512]{4,3,2,1,0:T(8,128)(2,1)S(1)}, bf16[1,4,1,80,512]{4,3,2,1,0:T(8,128)(2,1)S(1)}, u32[]{:S(2)}, u32[]{:S(2)}) %collective-permute-start.1) | collective-permute-done | bytes 327712 | tf_op jit(solution)/shard_map/ppermute | solution.py:18
  95.6 4.1 collective-permute-done.2
  99.7 1.2 pad_maximum_fusion
  101.0 0.2 reduce-scatter.5.cloned.1.call-start
  101.2 18.5 %all-gather.4.cloned.1.call-done = bf16[2,4,4,80,512]{4,3,2,1,0:T(8,128)(2,1)} async-done(((bf16[1,4,4,80,512]{4,3,2,1,0:T(8,128)(2,1)}), bf16[2,4,4,80,512]{4,3,2,1,0:T(8,128)(2,1)}) %all-gather.4.cloned.1.call-update) | async-done | bytes 2621456 | tf_op jit(solution)/shard_map/all_gather | solution.py:83
  119.7 1.4 slice_dynamic-update-slice_fusion.26
  121.0 1.1 slice_dynamic-update-slice_fusion.8
  122.2 1.2 slice_dynamic-update-slice_fusion.25
  123.4 0.2 slice_dynamic-update-slice_fusion.24
  123.6 0.2 slice_dynamic-update-slice_fusion.23
  123.8 0.2 slice_dynamic-update-slice_fusion.22
  124.0 0.2 slice_dynamic-update-slice_fusion.21
  124.4 0.2 slice_dynamic-update-slice_fusion.19
  124.5 0.2 slice_dynamic-update-slice_fusion.18
  124.8 0.2 slice_dynamic-update-slice_fusion.17
  125.1 0.2 slice_dynamic-update-slice_fusion.15
  125.5 0.2 slice_dynamic-update-slice_fusion.13
  125.9 0.2 slice_dynamic-update-slice_fusion.11
  126.3 0.2 slice_dynamic-update-slice_fusion.9
  126.4 6.1 %copy-done.3 = bf16[2,2,2,80,13824]{4,3,2,1,0:T(8,128)(2,1)} copy-done((bf16[2,2,2,80,13824]{4,3,2,1,0:T(8,128)(2,1)}, bf16[2,2,2,80,13824]{4,3,2,1,0:T(8,128)(2,1)S(1)}, u32[]{:S(2)}) %copy-start.3) | copy-done | bytes 17694744
  132.5 9.0 %convolution_multiply_fusion = f32[13824,256]{1,0:T(8,128)} fusion(bf16[640,13824]{1,0:T(8,128)(2,1)S(1)} %bitcast.46, bf16[640,256]{1,0:T(8,128)(2,1)S(1)} %bitcast.37), kind=kOutput, calls=%fused_computation | convolution fusion | flops 4533387264 | bytes 32178176 | tf_op jit(solution)/shard_map/dot_general | solution.py:91
  141.6 77.3 %all-reduce.2 = (f32[512]{0:T(512)}, f32[512]{0:T(512)}) all-reduce(f32[512]{0:T(512)S(1)} %broadcast_multiply_fusion.1, f32[512]{0:T(512)S(1)} %broadcast_multiply_fusion), channel_id=1, replica_groups=mesh['dp'=2,'tm'=32,'space'=4] {'dp','tm','space'}, use_global_device_ids=true, to_apply=%region_6.7 | all-reduce | flops 1024 | bytes 8192 | tf_op jit(solution)/shard_map/psum | solution.py:115
  218.8 165.5 %reduce-scatter.5.cloned.1.call-done = f32[432,256]{1,0:T(8,128)} async-done(((f32[13824,256]{1,0:T(8,128)}), f32[432,256]{1,0:T(8,128)}) %reduce-scatter.5.cloned.1.call-update) | async-done | bytes 442384 | tf_op jit(solution)/shard_map/reduce_scatter | solution.py:116
  384.3 10.5 %fusion = f32[2,2,2,80,256]{4,3,2,1,0:T(8,128)S(1)} fusion(bf16[2,2,2,80,13824]{4,3,2,1,0:T(8,128)(2,1)} %copy-done.3, bf16[13824,256]{1,0:T(8,128)(2,1)} %param.7), kind=kOutput, calls=%fused_computation.1 | convolution fusion | flops 4529848320 | bytes 25427968 | tf_op jit(solution)/shard_map/dot_general | solution.py:86
  394.9 4.3 %all_to_all.37 = f32[2,2,2,80,256]{4,3,2,1,0:T(8,128)S(1)} all-to-all(f32[2,2,2,80,256]{4,3,2,1,0:T(8,128)S(1)} %fusion), channel_id=1, replica_groups=mesh['dp'=2,'tm'=32,'space'=4] {'dp'}, dimensions={0} | all-to-all | bytes 1310720 | tf_op jit(solution)/shard_map/all_to_all | solution.py:88
  399.2 0.8 fusion.26
  400.0 15.8 %all-gather.6.cloned.1.call-done = f32[1728,256]{1,0:T(8,128)} async-done(((f32[432,256]{1,0:T(8,128)}), f32[1728,256]{1,0:T(8,128)}) %all-gather.6.cloned.1.call-update) | async-done | bytes 1769488 | tf_op jit(solution)/shard_map/all_gather | solution.py:117
  415.9 2.4 reduce_sum.47
  (71 shorter events, 2.9 us)
Async XLA Ops:
  7.2 62.9 %reduce-scatter.3.cloned.1.call-start = ((), (), s32[]{:S(2)}) async-start(), calls=%async_computation.5 | async-start | bytes 1966080 | tf_op jit(solution)/shard_map/reduce_scatter | solution.py:105
  13.0 11.6 %collective-permute-start.3 = (bf16[2,2,2,80,256]{4,3,2,1,0:T(8,128)(2,1)S(1)}, bf16[2,2,2,80,256]{4,3,2,1,0:T(8,128)(2,1)S(1)}, u32[]{:S(2)}, u32[]{:S(2)}) collective-permute-start(bf16[2,2,2,80,256]{4,3,2,1,0:T(8,128)(2,1)S(1)} %bitcast.32), channel_id=1, source_target_pairs={{4,0},{8,4},{12,8},{16,12},{20,16},{24,20},{28,24},{32,28},{36,32}... | collective-permute-start | bytes 983048 | tf_op jit(solution)/shard_map/ppermute | solution.py:10
  24.7 15.0 %collective-permute-start.4 = (bf16[2,4,1,80,256]{4,3,2,1,0:T(8,128)(2,1)S(1)}, bf16[2,4,1,80,256]{4,3,2,1,0:T(8,128)(2,1)S(1)}, u32[]{:S(2)}, u32[]{:S(2)}) collective-permute-start(bf16[2,4,1,80,256]{4,3,2,1,0:T(8,128)(2,1)S(1)} %get-tuple-element.11), channel_id=1, source_target_pairs={{0,1},{1,2},{2,3},{4,5},{5,6},{6,7},{8,9},{9,10},{10,11},{12,13},{... | collective-permute-start | bytes 983048 | tf_op jit(solution)/shard_map/ppermute | solution.py:18
  28.2 11.6 %collective-permute-start.5 = (bf16[2,4,1,80,256]{4,3,2,1,0:T(8,128)(2,1)S(1)}, bf16[2,4,1,80,256]{4,3,2,1,0:T(8,128)(2,1)S(1)}, u32[]{:S(2)}, u32[]{:S(2)}) collective-permute-start(bf16[2,4,1,80,256]{4,3,2,1,0:T(8,128)(2,1)S(1)} %get-tuple-element.12), channel_id=1, source_target_pairs={{1,0},{2,1},{3,2},{5,4},{6,5},{7,6},{9,8},{10,9},{11,10},{13,12},{... | collective-permute-start | bytes 983048 | tf_op jit(solution)/shard_map/ppermute | solution.py:21
  40.7 2.2 slice-start
  41.4 2.6 slice-start.1
  44.0 5.9 %copy-start.1 = (bf16[1,2,2,80,512]{4,3,2,1,0:T(8,128)(2,1)S(1)}, bf16[1,2,2,80,512]{4,3,2,1,0:T(8,128)(2,1)}, u32[]{:S(2)}) copy-start(bf16[1,2,2,80,512]{4,3,2,1,0:T(8,128)(2,1)} %param.5) | copy-start | bytes 983044
  44.0 26.1 %copy-start.4 = (f32[512]{0:T(512)S(1)}, f32[512]{0:T(512)}, u32[]{:S(2)}) copy-start(f32[512]{0:T(512)} %param.6) | copy-start | bytes 6148
  44.0 27.7 %copy-start.2 = (bf16[1,2,2,80,512]{4,3,2,1,0:T(8,128)(2,1)S(1)}, bf16[1,2,2,80,512]{4,3,2,1,0:T(8,128)(2,1)}, u32[]{:S(2)}) copy-start(bf16[1,2,2,80,512]{4,3,2,1,0:T(8,128)(2,1)} %param.9) | copy-start | bytes 983044
  49.8 69.8 %all-gather.4.cloned.1.call-start = ((), (), s32[]{:S(2)}) async-start(), calls=%async_computation.4 | async-start | bytes 3932160 | tf_op jit(solution)/shard_map/all_gather | solution.py:83
  74.1 11.6 %collective-permute-start = (bf16[1,2,2,80,512]{4,3,2,1,0:T(8,128)(2,1)S(1)}, bf16[1,2,2,80,512]{4,3,2,1,0:T(8,128)(2,1)S(1)}, u32[]{:S(2)}, u32[]{:S(2)}) collective-permute-start(bf16[1,2,2,80,512]{4,3,2,1,0:T(8,128)(2,1)S(1)} %get-tuple-element.16), channel_id=1, source_target_pairs={{0,4},{4,8},{8,12},{12,16},{16,20},{20,24},{24,28},{28,32},{32,36}... | collective-permute-start | bytes 983048 | tf_op jit(solution)/shard_map/ppermute | solution.py:10
  85.8 9.8 %collective-permute-start.1 = (bf16[1,4,1,80,512]{4,3,2,1,0:T(8,128)(2,1)S(1)}, bf16[1,4,1,80,512]{4,3,2,1,0:T(8,128)(2,1)S(1)}, u32[]{:S(2)}, u32[]{:S(2)}) collective-permute-start(bf16[1,4,1,80,512]{4,3,2,1,0:T(8,128)(2,1)S(1)} %get-tuple-element.13), channel_id=1, source_target_pairs={{0,1},{1,2},{2,3},{4,5},{5,6},{6,7},{8,9},{9,10},{10,11},{12,13},{... | collective-permute-start | bytes 983048 | tf_op jit(solution)/shard_map/ppermute | solution.py:18
  89.2 10.5 %collective-permute-start.2 = (bf16[1,4,1,80,512]{4,3,2,1,0:T(8,128)(2,1)S(1)}, bf16[1,4,1,80,512]{4,3,2,1,0:T(8,128)(2,1)S(1)}, u32[]{:S(2)}, u32[]{:S(2)}) collective-permute-start(bf16[1,4,1,80,512]{4,3,2,1,0:T(8,128)(2,1)S(1)} %get-tuple-element.14), channel_id=1, source_target_pairs={{1,0},{2,1},{3,2},{5,4},{6,5},{7,6},{9,8},{10,9},{11,10},{13,12},{... | collective-permute-start | bytes 983048 | tf_op jit(solution)/shard_map/ppermute | solution.py:21
  101.0 283.4 %reduce-scatter.5.cloned.1.call-start = ((), (), s32[]{:S(2)}) async-start(), calls=%async_computation.6 | async-start | bytes 14598144 | tf_op jit(solution)/shard_map/reduce_scatter | solution.py:116
  119.6 3.8 copy-start
  126.4 6.1 %copy-start.3 = (bf16[2,2,2,80,13824]{4,3,2,1,0:T(8,128)(2,1)}, bf16[2,2,2,80,13824]{4,3,2,1,0:T(8,128)(2,1)S(1)}, u32[]{:S(2)}) copy-start(bf16[2,2,2,80,13824]{4,3,2,1,0:T(8,128)(2,1)S(1)} %slice_dynamic-update-slice_fusion.9) | copy-start | bytes 53084164
  141.5 274.4 %all-gather.6.cloned.1.call-start = ((), (), s32[]{:S(2)}) async-start(), calls=%async_computation.7 | async-start | bytes 2211840 | tf_op jit(solution)/shard_map/all_gather | solution.py:117
  384.3 14.9 %copy-start.5 = (f32[512]{0:T(512)S(1)}, f32[512]{0:T(512)}, u32[]{:S(2)}) copy-start(f32[512]{0:T(512)} %param.8) | copy-start | bytes 6148
Sparse Core Ops, SparseCore 0:
  50.0 20.0 reduce-scatter.2
  101.1 18.5 all-gather.3
  141.6 242.6 reduce-scatter.4
  386.0 29.8 all-gather.5
